TPU v7x, 32 devices: a whole 2x2x4 slice. The times are simulated.
32 devices in a mesh: chan: 8 (over z, y), tm: 4 (over x, core).
Axes of the slice: x: 2, y: 2, z: 4, core: 2. Of those that a mesh axis runs over, the one named last changes fastest.
Arguments:
- record: bfloat16 [96, 2048], P('chan', 'tm'), may hold values from -6 to 6
- fir: float32 [96, 65], P('chan'), may hold values from -0.75 to 0.75
Outputs:
- xcorr: float32 [4, 96, 96, 256], P('tm', 'chan')
All inputs are finite; a program needn't handle non-finite values.
Results may differ from a plain program's by a relative error of at most 0.004.
Values may be sent and summed in bfloat16 or wider, within the bound.
A program may use at most 64 MiB of HBM per device.

v0:
```python
import math
import jax
import jax.numpy as jnp
from jax import lax
from jax.sharding import PartitionSpec as P

GROUP = 512
MAXLAG = 128


def extended_2(block, sides, width):
    for axis, dim in sides:
        count = lax.axis_size(axis)
        forward = [(i, i + 1) for i in range(count - 1)]
        backward = [(target, source) for source, target in forward]
        low = lax.ppermute(
            lax.slice_in_dim(block, block.shape[dim] - width, None, axis=dim), axis, forward
        )
        high = lax.ppermute(lax.slice_in_dim(block, 0, width, axis=dim), axis, backward)
        block = jnp.concatenate([low, block, high], axis=dim)
    return block


def whiten(widened_raw, fir, length):
    widened = widened_raw.astype(jnp.float32)
    running = jnp.zeros((widened.shape[0], length), jnp.float32)
    for k in range(fir.shape[1]):
        running = running + fir[:, k : k + 1] * widened[:, k : k + length]
    return running


def local(record, fir):
    ch_dev = record.shape[0]
    local_len = record.shape[1]
    half_width = (fir.shape[1] - 1) // 2
    lag_count = 2 * MAXLAG
    span = GROUP + lag_count
    factor = 1.0 / math.sqrt(GROUP)
    raw_ext = extended_2(record, (("tm", 1),), half_width)
    whitened = whiten(raw_ext, fir, local_len).astype(jnp.bfloat16)
    extended = extended_2(whitened, (("tm", 1),), MAXLAG)
    c = 0
    segment = extended[:, c * GROUP + MAXLAG : c * GROUP + MAXLAG + GROUP]
    padded = jnp.concatenate([segment, jnp.zeros((ch_dev, lag_count + 1), jnp.bfloat16)], axis=1)
    tiled = jnp.tile(padded, (1, lag_count))[:, : lag_count * span]
    expanded = [tiled.reshape(ch_dev, lag_count, span)]
    c = 0
    window = lax.all_gather(extended, "chan", axis=0, tiled=True)
    blocks = [
        jnp.einsum("amu,ju->ajm", expanded[c], window, preferred_element_type=jnp.float32) * factor
    ]
    return jnp.stack(blocks)


def solution(mesh):
    in_specs = (P("chan", "tm"), P("chan", None))
    out_specs = P("tm", "chan", None, None)
    return jax.shard_map(local, mesh=mesh, in_specs=in_specs, out_specs=out_specs, check_vma=False)
```

profile of v0, /device:TPU:6, one launch (start us, length us, event | category | flops | bytes accessed | tf_op | source)
XLA Modules:
  0.0 80.0 jit_solution(231138366995109417)
XLA Ops:
  0.0 0.8 fusion.74
  0.8 1.9 %collective-permute-start = (bf16[12,32]{1,0:T(8,128)(2,1)S(1)}, bf16[12,32]{1,0:T(8,128)(2,1)S(1)}, u32[]{:S(2)}, u32[]{:S(2)}) collective-permute-start(bf16[12,32]{1,0:T(8,128)(2,1)S(1)} %get-tuple-element.72), channel_id=1, source_target_pairs={{0,1},{1,2},{2,3},{4,5},{5,6},{6,7},{8,9},{9,10},{10,11},{12,13},{... | collective-permute-start | bytes 2312 | tf_op jit(solution)/shard_map/ppermute | solution.py:16
  2.7 3.6 %collective-permute-start.1 = (bf16[12,32]{1,0:T(8,128)(2,1)S(1)}, bf16[12,32]{1,0:T(8,128)(2,1)S(1)}, u32[]{:S(2)}, u32[]{:S(2)}) collective-permute-start(bf16[12,32]{1,0:T(8,128)(2,1)S(1)} %get-tuple-element.73), channel_id=1, source_target_pairs={{1,0},{2,1},{3,2},{5,4},{6,5},{7,6},{9,8},{10,9},{11,10},{13,12},{... | collective-permute-start | bytes 2312 | tf_op jit(solution)/shard_map/ppermute | solution.py:19
  6.3 1.9 %slice_reduce_fusion.64 = (f32[12]{0:T(128)S(1)}, f32[12]{0:T(128)S(1)}, f32[12]{0:T(128)S(1)}, f32[12]{0:T(128)S(1)}, f32[12]{0:T(128)S(1)}, /*index=5*/f32[12]...) fusion(f32[12,65]{1,0:T(8,128)} %param.3), kind=kLoop, calls=%fused_computation.200 | loop fusion | bytes 1824 | tf_op jit(solution)/shard_map/slice | solution.py:28
  8.3 1.9 %slice_reduce_fusion.63 = (f32[12]{0:T(128)S(1)}, f32[12]{0:T(128)S(1)}, f32[12]{0:T(128)S(1)}, f32[12]{0:T(128)S(1)}, f32[12]{0:T(128)S(1)}, /*index=5*/f32[12]...) fusion(f32[12,65]{1,0:T(8,128)} %param.3), kind=kLoop, calls=%fused_computation.199 | loop fusion | bytes 1824 | tf_op jit(solution)/shard_map/slice | solution.py:28
  10.2 1.9 %slice_reduce_fusion.62 = (f32[12]{0:T(128)S(1)}, f32[12]{0:T(128)S(1)}, f32[12]{0:T(128)S(1)}, f32[12]{0:T(128)S(1)}, f32[12]{0:T(128)S(1)}, /*index=5*/f32[12]...) fusion(f32[12,65]{1,0:T(8,128)} %param.3), kind=kLoop, calls=%fused_computation.198 | loop fusion | bytes 1824 | tf_op jit(solution)/shard_map/slice | solution.py:28
  12.1 1.3 %slice_reduce_fusion.61 = (f32[12]{0:T(128)S(1)}, f32[12]{0:T(128)S(1)}, f32[12]{0:T(128)S(1)}, f32[12]{0:T(128)S(1)}, f32[12]{0:T(128)S(1)}, /*index=5*/f32[12]{0:T(128)S(1)}, f32[12]{0:T(128)S(1)}, f32[12]{0:T(128)S(1)}) fusion(f32[12,65]{1,0:T(8,128)} %param.3), kind=kLoop, calls=%fused_computation.197 | loop fusion | bytes 768 | tf_op jit(solution)/shard_map/slice | solution.py:28
  13.4 0.0 collective-permute-done
  13.5 0.0 collective-permute-done.1
  13.5 0.8 maximum_convert_fusion
  14.3 0.8 fusion.9
  15.1 1.9 %collective-permute-start.2 = (bf16[12,128]{1,0:T(8,128)(2,1)S(1)}, bf16[12,128]{1,0:T(8,128)(2,1)S(1)}, u32[]{:S(2)}, u32[]{:S(2)}) collective-permute-start(bf16[12,128]{1,0:T(8,128)(2,1)S(1)} %get-tuple-element.70), channel_id=1, source_target_pairs={{0,1},{1,2},{2,3},{4,5},{5,6},{6,7},{8,9},{9,10},{10,11},{12,13},{... | collective-permute-start | bytes 9224 | tf_op jit(solution)/shard_map/ppermute | solution.py:16
  17.0 3.6 %collective-permute-start.3 = (bf16[12,128]{1,0:T(8,128)(2,1)S(1)}, bf16[12,128]{1,0:T(8,128)(2,1)S(1)}, u32[]{:S(2)}, u32[]{:S(2)}) collective-permute-start(bf16[12,128]{1,0:T(8,128)(2,1)S(1)} %get-tuple-element.71), channel_id=1, source_target_pairs={{1,0},{2,1},{3,2},{5,4},{6,5},{7,6},{9,8},{10,9},{11,10},{13,12},{... | collective-permute-start | bytes 9224 | tf_op jit(solution)/shard_map/ppermute | solution.py:19
  20.7 2.9 %tile.4 = bf16[12,256,769]{2,1,0:T(8,128)(2,1)} broadcast(bf16[12,769]{1,0:T(8,128)(2,1)S(1)} %concatenate.11), dimensions={0,2} | broadcast | bytes 4743192 | tf_op jit(solution)/shard_map/tile | solution.py:45
  23.5 13.6 %tile.10 = bf16[12,196864]{1,0:T(8,128)(2,1)} reshape(bf16[12,256,769]{2,1,0:T(8,128)(2,1)} %tile.4) | data formatting | bytes 9449472 | tf_op jit(solution)/shard_map/tile | solution.py:45
  37.1 0.0 slice-start
  37.1 2.8 %slice-done = bf16[12,196608]{1,0:T(8,128)(2,1)S(1)} async-done(((bf16[12,196864]{1,0:T(8,128)(2,1)}), bf16[12,196608]{1,0:T(8,128)(2,1)S(1)}, s32[]{:S(2)}) %slice-start) | async-done | bytes 4718616 | tf_op jit(solution)/shard_map/slice | solution.py:45
  39.9 4.1 %copy.3 = bf16[2,8,256,768]{3,2,1,0:T(8,128)(2,1)} copy(bf16[2,8,256,768]{3,1,2,0:T(8,128)(2,1)S(1)} %bitcast.10) | data formatting | bytes 12582912
  44.0 0.0 collective-permute-done.2
  44.0 0.0 collective-permute-done.3
  44.0 31.0 %all-gather = bf16[8,12,768]{2,1,0:T(8,128)(2,1)S(1)} all-gather(bf16[1,12,768]{2,1,0:T(8,128)(2,1)S(1)} %maximum_bitcast_fusion), channel_id=1, replica_groups=mesh['chan'=8,'tm'=4] {'chan'}, dimensions={0}, use_global_device_ids=true | all-gather | bytes 165888 | tf_op jit(solution)/shard_map/all_gather | solution.py:48
  75.1 4.9 %fusion.5 = f32[1,12,96,256]{3,2,1,0:T(8,128)} fusion(bf16[96,768,1]{1,0,2:T(8,128)(2,1)S(1)} %reshape.10, bf16[16,256,768]{2,1,0:T(8,128)(2,1)} %bitcast.11), kind=kOutput, calls=%fused_computation.3 | convolution fusion | flops 453279744 | bytes 6045696 | tf_op jit(solution)/shard_map/amu,ju->ajm/dot_general | solution.py:50
  (4 shorter events, 0.1 us)
Async XLA Ops:
  0.8 12.7 %collective-permute-start = (bf16[12,32]{1,0:T(8,128)(2,1)S(1)}, bf16[12,32]{1,0:T(8,128)(2,1)S(1)}, u32[]{:S(2)}, u32[]{:S(2)}) collective-permute-start(bf16[12,32]{1,0:T(8,128)(2,1)S(1)} %get-tuple-element.72), channel_id=1, source_target_pairs={{0,1},{1,2},{2,3},{4,5},{5,6},{6,7},{8,9},{9,10},{10,11},{12,13},{... | collective-permute-start | bytes 2312 | tf_op jit(solution)/shard_map/ppermute | solution.py:16
  2.7 10.8 %collective-permute-start.1 = (bf16[12,32]{1,0:T(8,128)(2,1)S(1)}, bf16[12,32]{1,0:T(8,128)(2,1)S(1)}, u32[]{:S(2)}, u32[]{:S(2)}) collective-permute-start(bf16[12,32]{1,0:T(8,128)(2,1)S(1)} %get-tuple-element.73), channel_id=1, source_target_pairs={{1,0},{2,1},{3,2},{5,4},{6,5},{7,6},{9,8},{10,9},{11,10},{13,12},{... | collective-permute-start | bytes 2312 | tf_op jit(solution)/shard_map/ppermute | solution.py:19
  15.1 28.9 %collective-permute-start.2 = (bf16[12,128]{1,0:T(8,128)(2,1)S(1)}, bf16[12,128]{1,0:T(8,128)(2,1)S(1)}, u32[]{:S(2)}, u32[]{:S(2)}) collective-permute-start(bf16[12,128]{1,0:T(8,128)(2,1)S(1)} %get-tuple-element.70), channel_id=1, source_target_pairs={{0,1},{1,2},{2,3},{4,5},{5,6},{6,7},{8,9},{9,10},{10,11},{12,13},{... | collective-permute-start | bytes 9224 | tf_op jit(solution)/shard_map/ppermute | solution.py:16
  17.0 27.0 %collective-permute-start.3 = (bf16[12,128]{1,0:T(8,128)(2,1)S(1)}, bf16[12,128]{1,0:T(8,128)(2,1)S(1)}, u32[]{:S(2)}, u32[]{:S(2)}) collective-permute-start(bf16[12,128]{1,0:T(8,128)(2,1)S(1)} %get-tuple-element.71), channel_id=1, source_target_pairs={{1,0},{2,1},{3,2},{5,4},{6,5},{7,6},{9,8},{10,9},{11,10},{13,12},{... | collective-permute-start | bytes 9224 | tf_op jit(solution)/shard_map/ppermute | solution.py:19
  37.1 2.8 %slice-start = ((bf16[12,196864]{1,0:T(8,128)(2,1)}), bf16[12,196608]{1,0:T(8,128)(2,1)S(1)}, s32[]{:S(2)}) async-start(bf16[12,196864]{1,0:T(8,128)(2,1)} %tile.10), calls=%async_computation | async-start | bytes 12582912 | tf_op jit(solution)/shard_map/slice | solution.py:45
where the time goes:
time: 80.6 us; the launch traced here: 80 us
  local copies, waits for them, and re-layouts  31.2 us (39%)
  blocking collectives  31 us (38%)
  starting transfers between devices  11.1 us (14%)
  matrix products  4.89 us (6%)
  other arithmetic  1.59 us (2%)
    all_gather x1, blocking collectives, local(): window = lax.all_gather(extended, 'chan', axis=0, tiled=True)  31 us
    another operation x2, local copies, waits for them, and re-layouts, local(): tiled = jnp.tile(padded, (1, lag_count))[:, :lag_count * span]  16.5 us
    ppermute x2, starting transfers between devices, extended_2(): lax.ppermute(lax.slice_in_dim(block, 0, width, axis=dim), axis, backward)  7.28 us
    slice x4, local copies, waits for them, and re-layouts, whiten(): running = running + fir[:, k:k + 1] * widened[:, k:k + length]  7.1 us
    dot_general x1, matrix products, local(): jnp.einsum('amu,ju->ajm', expanded[c], window, preferred_element_type=jnp...  4.89 us
    unnamed x2, local copies, waits for them, and re-layouts  4.09 us
    ppermute x2, starting transfers between devices, extended_2(): lax.ppermute(lax.slice_in_dim(block, block.shape[dim] - width, None, axis...  3.83 us
    slice x2, local copies, waits for them, and re-layouts, local(): tiled = jnp.tile(padded, (1, lag_count))[:, :lag_count * span]  2.78 us
  transfers between devices with their start and end apart: 4, of which 0 were waited for; matrix products, arithmetic and copies ran while one was open for 35% of the time, Pallas kernels for 0%

commit v1 on v0

--- a/solution.py
+++ b/solution.py
@@ -45,7 +45,17 @@
     tiled = jnp.tile(padded, (1, lag_count))[:, : lag_count * span]
     expanded = [tiled.reshape(ch_dev, lag_count, span)]
     c = 0
-    window = lax.all_gather(extended, "chan", axis=0, tiled=True)
+    total_devices = lax.axis_size("chan")
+    fields = [extended]
+    dev_j = 0
+    while dev_j < total_devices - 1:
+        seen_now = lax.ppermute(
+            fields[-1], "chan", [(ii, (ii + 1) % total_devices) for ii in range(total_devices)]
+        )
+        fields.append(seen_now)
+        dev_j += 1
+    out_arr = jnp.concatenate(fields[::-1], axis=0)
+    window = jnp.roll(out_arr, (lax.axis_index("chan") + 1) * extended.shape[0], axis=0)
     blocks = [
         jnp.einsum("amu,ju->ajm", expanded[c], window, preferred_element_type=jnp.float32) * factor
     ]

time: 80.6 us -> 91.8 us (1.14)
  the two profiles are of different devices: /device:TPU:6 before, /device:TPU:0 now
where the time goes in v1:
time: 91.8 us; the launch traced here: 91.1 us
  waiting for transfers between devices  40.6 us (44%)
  local copies, waits for them, and re-layouts  32.3 us (35%)
  starting transfers between devices  11.6 us (13%)
  matrix products  4.9 us (5%)
  other arithmetic  1.59 us (2%)
    ppermute x7, waiting for transfers between devices, local(): lax.ppermute(fields[-1], 'chan', [(ii, (ii + 1) % total_devices) for ii i...  37.6 us
    another operation x2, local copies, waits for them, and re-layouts, local(): tiled = jnp.tile(padded, (1, lag_count))[:, :lag_count * span]  16.5 us
    ppermute x2, starting transfers between devices, extended_2(): lax.ppermute(lax.slice_in_dim(block, block.shape[dim] - width, None, axis...  7.48 us
    slice x4, local copies, waits for them, and re-layouts, whiten(): running = running + fir[:, k:k + 1] * widened[:, k:k + length]  7.1 us
    dot_general x1, matrix products, local(): jnp.einsum('amu,ju->ajm', expanded[c], window, preferred_element_type=jnp...  4.9 us
    unnamed x1, local copies, waits for them, and re-layouts  4.05 us
    ppermute x2, waiting for transfers between devices, extended_2(): lax.ppermute(lax.slice_in_dim(block, 0, width, axis=dim), axis, backward)  2.99 us
    slice x2, local copies, waits for them, and re-layouts, local(): tiled = jnp.tile(padded, (1, lag_count))[:, :lag_count * span]  2.78 us
  transfers between devices with their start and end apart: 11, of which 7 were waited for; matrix products, arithmetic and copies ran while one was open for 30% of the time, Pallas kernels for 0%

profile of v1, /device:TPU:0, one launch (start us, length us, event | category | flops | bytes accessed | tf_op | source)
XLA Modules:
  0.0 91.1 jit_solution(11939581738660626679)
XLA Ops:
  0.8 2.3 %collective-permute-start = (bf16[12,32]{1,0:T(8,128)(2,1)S(1)}, bf16[12,32]{1,0:T(8,128)(2,1)S(1)}, u32[]{:S(2)}, u32[]{:S(2)}) collective-permute-start(bf16[12,32]{1,0:T(8,128)(2,1)S(1)} %get-tuple-element.72), channel_id=1, source_target_pairs={{0,1},{1,2},{2,3},{4,5},{5,6},{6,7},{8,9},{9,10},{10,11},{12,13},{... | collective-permute-start | bytes 2312 | tf_op jit(solution)/shard_map/ppermute | solution.py:16
  3.1 1.3 %collective-permute-start.1 = (bf16[12,32]{1,0:T(8,128)(2,1)S(1)}, bf16[12,32]{1,0:T(8,128)(2,1)S(1)}, u32[]{:S(2)}, u32[]{:S(2)}) collective-permute-start(bf16[12,32]{1,0:T(8,128)(2,1)S(1)} %get-tuple-element.73), channel_id=1, source_target_pairs={{1,0},{2,1},{3,2},{5,4},{6,5},{7,6},{9,8},{10,9},{11,10},{13,12},{... | collective-permute-start | bytes 2312 | tf_op jit(solution)/shard_map/ppermute | solution.py:19
  4.4 1.9 %slice_reduce_fusion.64 = (f32[12]{0:T(128)S(1)}, f32[12]{0:T(128)S(1)}, f32[12]{0:T(128)S(1)}, f32[12]{0:T(128)S(1)}, f32[12]{0:T(128)S(1)}, /*index=5*/f32[12]...) fusion(f32[12,65]{1,0:T(8,128)} %param.3), kind=kLoop, calls=%fused_computation.202 | loop fusion | bytes 1824 | tf_op jit(solution)/shard_map/slice | solution.py:28
  6.4 1.9 %slice_reduce_fusion.63 = (f32[12]{0:T(128)S(1)}, f32[12]{0:T(128)S(1)}, f32[12]{0:T(128)S(1)}, f32[12]{0:T(128)S(1)}, f32[12]{0:T(128)S(1)}, /*index=5*/f32[12]...) fusion(f32[12,65]{1,0:T(8,128)} %param.3), kind=kLoop, calls=%fused_computation.201 | loop fusion | bytes 1824 | tf_op jit(solution)/shard_map/slice | solution.py:28
  8.3 1.9 %slice_reduce_fusion.62 = (f32[12]{0:T(128)S(1)}, f32[12]{0:T(128)S(1)}, f32[12]{0:T(128)S(1)}, f32[12]{0:T(128)S(1)}, f32[12]{0:T(128)S(1)}, /*index=5*/f32[12]...) fusion(f32[12,65]{1,0:T(8,128)} %param.3), kind=kLoop, calls=%fused_computation.200 | loop fusion | bytes 1824 | tf_op jit(solution)/shard_map/slice | solution.py:28
  10.2 1.3 %slice_reduce_fusion.61 = (f32[12]{0:T(128)S(1)}, f32[12]{0:T(128)S(1)}, f32[12]{0:T(128)S(1)}, f32[12]{0:T(128)S(1)}, f32[12]{0:T(128)S(1)}, /*index=5*/f32[12]{0:T(128)S(1)}, f32[12]{0:T(128)S(1)}, f32[12]{0:T(128)S(1)}) fusion(f32[12,65]{1,0:T(8,128)} %param.3), kind=kLoop, calls=%fused_computation.199 | loop fusion | bytes 768 | tf_op jit(solution)/shard_map/slice | solution.py:28
  11.6 0.8 maximum_convert_fusion
  12.3 0.8 fusion.11
  13.2 5.1 %collective-permute-start.2 = (bf16[12,128]{1,0:T(8,128)(2,1)S(1)}, bf16[12,128]{1,0:T(8,128)(2,1)S(1)}, u32[]{:S(2)}, u32[]{:S(2)}) collective-permute-start(bf16[12,128]{1,0:T(8,128)(2,1)S(1)} %get-tuple-element.70), channel_id=1, source_target_pairs={{0,1},{1,2},{2,3},{4,5},{5,6},{6,7},{8,9},{9,10},{10,11},{12,13},{... | collective-permute-start | bytes 9224 | tf_op jit(solution)/shard_map/ppermute | solution.py:16
  18.3 1.3 %collective-permute-start.3 = (bf16[12,128]{1,0:T(8,128)(2,1)S(1)}, bf16[12,128]{1,0:T(8,128)(2,1)S(1)}, u32[]{:S(2)}, u32[]{:S(2)}) collective-permute-start(bf16[12,128]{1,0:T(8,128)(2,1)S(1)} %get-tuple-element.71), channel_id=1, source_target_pairs={{1,0},{2,1},{3,2},{5,4},{6,5},{7,6},{9,8},{10,9},{11,10},{13,12},{... | collective-permute-start | bytes 9224 | tf_op jit(solution)/shard_map/ppermute | solution.py:19
  19.6 3.0 %collective-permute-done.3 = bf16[12,128]{1,0:T(8,128)(2,1)S(1)} collective-permute-done((bf16[12,128]{1,0:T(8,128)(2,1)S(1)}, bf16[12,128]{1,0:T(8,128)(2,1)S(1)}, u32[]{:S(2)}, u32[]{:S(2)}) %collective-permute-start.3) | collective-permute-done | bytes 3104 | tf_op jit(solution)/shard_map/ppermute | solution.py:19
  22.6 1.5 %collective-permute-start.4 = (bf16[12,768]{1,0:T(8,128)(2,1)S(1)}, bf16[12,768]{1,0:T(8,128)(2,1)S(1)}, u32[]{:S(2)}, u32[]{:S(2)}) collective-permute-start(bf16[12,768]{1,0:T(8,128)(2,1)S(1)} %pad_maximum_fusion), channel_id=1, source_target_pairs={{0,4},{4,8},{8,12},{12,16},{16,20},{20,24},{24,28},{28,0},{1,5},{5... | collective-permute-start | bytes 55304 | tf_op jit(solution)/shard_map/ppermute | solution.py:52
  24.1 5.0 %collective-permute-done.4 = bf16[12,768]{1,0:T(8,128)(2,1)S(1)} collective-permute-done((bf16[12,768]{1,0:T(8,128)(2,1)S(1)}, bf16[12,768]{1,0:T(8,128)(2,1)S(1)}, u32[]{:S(2)}, u32[]{:S(2)}) %collective-permute-start.4) | collective-permute-done | bytes 18464 | tf_op jit(solution)/shard_map/ppermute | solution.py:52
  29.1 6.5 %collective-permute-done.5 = bf16[12,768]{1,0:T(8,128)(2,1)S(1)} collective-permute-done((bf16[12,768]{1,0:T(8,128)(2,1)S(1)}, bf16[12,768]{1,0:T(8,128)(2,1)S(1)}, u32[]{:S(2)}, u32[]{:S(2)}) %collective-permute-start.5) | collective-permute-done | bytes 18464 | tf_op jit(solution)/shard_map/ppermute | solution.py:52
  35.7 6.5 %collective-permute-done.6 = bf16[12,768]{1,0:T(8,128)(2,1)S(1)} collective-permute-done((bf16[12,768]{1,0:T(8,128)(2,1)S(1)}, bf16[12,768]{1,0:T(8,128)(2,1)S(1)}, u32[]{:S(2)}, u32[]{:S(2)}) %collective-permute-start.6) | collective-permute-done | bytes 18464 | tf_op jit(solution)/shard_map/ppermute | solution.py:52
  42.2 6.5 %collective-permute-done.7 = bf16[12,768]{1,0:T(8,128)(2,1)S(1)} collective-permute-done((bf16[12,768]{1,0:T(8,128)(2,1)S(1)}, bf16[12,768]{1,0:T(8,128)(2,1)S(1)}, u32[]{:S(2)}, u32[]{:S(2)}) %collective-permute-start.7) | collective-permute-done | bytes 18464 | tf_op jit(solution)/shard_map/ppermute | solution.py:52
  48.7 6.5 %collective-permute-done.8 = bf16[12,768]{1,0:T(8,128)(2,1)S(1)} collective-permute-done((bf16[12,768]{1,0:T(8,128)(2,1)S(1)}, bf16[12,768]{1,0:T(8,128)(2,1)S(1)}, u32[]{:S(2)}, u32[]{:S(2)}) %collective-permute-start.8) | collective-permute-done | bytes 18464 | tf_op jit(solution)/shard_map/ppermute | solution.py:52
  55.2 6.5 %collective-permute-done.9 = bf16[12,768]{1,0:T(8,128)(2,1)S(1)} collective-permute-done((bf16[12,768]{1,0:T(8,128)(2,1)S(1)}, bf16[12,768]{1,0:T(8,128)(2,1)S(1)}, u32[]{:S(2)}, u32[]{:S(2)}) %collective-permute-start.9) | collective-permute-done | bytes 18464 | tf_op jit(solution)/shard_map/ppermute | solution.py:52
  61.8 2.9 %tile.4 = bf16[12,256,769]{2,1,0:T(8,128)(2,1)} broadcast(bf16[12,769]{1,0:T(8,128)(2,1)S(1)} %concatenate.18), dimensions={0,2} | broadcast | bytes 4743192 | tf_op jit(solution)/shard_map/tile | solution.py:45
  64.6 13.6 %tile.10 = bf16[12,196864]{1,0:T(8,128)(2,1)} reshape(bf16[12,256,769]{2,1,0:T(8,128)(2,1)} %tile.4) | data formatting | bytes 9449472 | tf_op jit(solution)/shard_map/tile | solution.py:45
  78.2 2.8 %slice-done = bf16[12,196608]{1,0:T(8,128)(2,1)S(1)} async-done(((bf16[12,196864]{1,0:T(8,128)(2,1)}), bf16[12,196608]{1,0:T(8,128)(2,1)S(1)}, s32[]{:S(2)}) %slice-start) | async-done | bytes 4718616 | tf_op jit(solution)/shard_map/slice | solution.py:45
  81.0 4.1 %copy.3 = bf16[2,8,256,768]{3,2,1,0:T(8,128)(2,1)} copy(bf16[2,8,256,768]{3,1,2,0:T(8,128)(2,1)S(1)} %bitcast.10) | data formatting | bytes 12582912
  85.1 1.1 %concatenate.17 = bf16[192,768]{1,0:T(8,128)(2,1)S(1)} concatenate(bf16[12,768]{1,0:T(8,128)(2,1)S(1)} %collective-permute-done.10, bf16[12,768]{1,0:T(8,128)(2,1)S(1)} %collective-permute-done.9, bf16[12,768]{1,0:T(8,128)(2,1)S(1)} %collective-permute-done.8, bf16[12,768]{1,0:T(8,128)(2,1)S(1)} %collective-permute-done.7, bf16[12,768]{1,0:T(8,128)(2,1)S(1)} %collective-permute-done.6, ...), dimensions={0} | concatenate | bytes 589824 | tf_op jit(solution)/shard_map/jit(_roll_dynamic)/concatenate | solution.py:58
  86.2 4.9 %fusion.5 = f32[1,12,96,256]{3,2,1,0:T(8,128)} fusion(bf16[16,256,768]{2,1,0:T(8,128)(2,1)} %bitcast.11, bf16[192,768]{1,0:T(8,128)(2,1)S(1)} %concatenate.17, s32[]{:T(128)S(6)} %select_n.14), kind=kOutput, calls=%fused_computation.3 | convolution fusion | flops 453279744 | bytes 6045700 | tf_op jit(solution)/shard_map/amu,ju->ajm/dot_general | solution.py:60
  (15 shorter events, 0.8 us)
Async XLA Ops:
  0.8 10.8 %collective-permute-start = (bf16[12,32]{1,0:T(8,128)(2,1)S(1)}, bf16[12,32]{1,0:T(8,128)(2,1)S(1)}, u32[]{:S(2)}, u32[]{:S(2)}) collective-permute-start(bf16[12,32]{1,0:T(8,128)(2,1)S(1)} %get-tuple-element.72), channel_id=1, source_target_pairs={{0,1},{1,2},{2,3},{4,5},{5,6},{6,7},{8,9},{9,10},{10,11},{12,13},{... | collective-permute-start | bytes 2312 | tf_op jit(solution)/shard_map/ppermute | solution.py:16
  3.1 8.4 %collective-permute-start.1 = (bf16[12,32]{1,0:T(8,128)(2,1)S(1)}, bf16[12,32]{1,0:T(8,128)(2,1)S(1)}, u32[]{:S(2)}, u32[]{:S(2)}) collective-permute-start(bf16[12,32]{1,0:T(8,128)(2,1)S(1)} %get-tuple-element.73), channel_id=1, source_target_pairs={{1,0},{2,1},{3,2},{5,4},{6,5},{7,6},{9,8},{10,9},{11,10},{13,12},{... | collective-permute-start | bytes 2312 | tf_op jit(solution)/shard_map/ppermute | solution.py:19
  13.2 6.4 %collective-permute-start.2 = (bf16[12,128]{1,0:T(8,128)(2,1)S(1)}, bf16[12,128]{1,0:T(8,128)(2,1)S(1)}, u32[]{:S(2)}, u32[]{:S(2)}) collective-permute-start(bf16[12,128]{1,0:T(8,128)(2,1)S(1)} %get-tuple-element.70), channel_id=1, source_target_pairs={{0,1},{1,2},{2,3},{4,5},{5,6},{6,7},{8,9},{9,10},{10,11},{12,13},{... | collective-permute-start | bytes 9224 | tf_op jit(solution)/shard_map/ppermute | solution.py:16
  18.3 4.3 %collective-permute-start.3 = (bf16[12,128]{1,0:T(8,128)(2,1)S(1)}, bf16[12,128]{1,0:T(8,128)(2,1)S(1)}, u32[]{:S(2)}, u32[]{:S(2)}) collective-permute-start(bf16[12,128]{1,0:T(8,128)(2,1)S(1)} %get-tuple-element.71), channel_id=1, source_target_pairs={{1,0},{2,1},{3,2},{5,4},{6,5},{7,6},{9,8},{10,9},{11,10},{13,12},{... | collective-permute-start | bytes 9224 | tf_op jit(solution)/shard_map/ppermute | solution.py:19
  22.6 6.5 %collective-permute-start.4 = (bf16[12,768]{1,0:T(8,128)(2,1)S(1)}, bf16[12,768]{1,0:T(8,128)(2,1)S(1)}, u32[]{:S(2)}, u32[]{:S(2)}) collective-permute-start(bf16[12,768]{1,0:T(8,128)(2,1)S(1)} %pad_maximum_fusion), channel_id=1, source_target_pairs={{0,4},{4,8},{8,12},{12,16},{16,20},{20,24},{24,28},{28,0},{1,5},{5... | collective-permute-start | bytes 55304 | tf_op jit(solution)/shard_map/ppermute | solution.py:52
  29.1 6.5 %collective-permute-start.5 = (bf16[12,768]{1,0:T(8,128)(2,1)S(1)}, bf16[12,768]{1,0:T(8,128)(2,1)S(1)}, u32[]{:S(2)}, u32[]{:S(2)}) collective-permute-start(bf16[12,768]{1,0:T(8,128)(2,1)S(1)} %collective-permute-done.4), channel_id=1, source_target_pairs={{0,4},{4,8},{8,12},{12,16},{16,20},{20,24},{24,28},{28,0},{1,5},{5... | collective-permute-start | bytes 55304 | tf_op jit(solution)/shard_map/ppermute | solution.py:52
  35.7 6.5 %collective-permute-start.6 = (bf16[12,768]{1,0:T(8,128)(2,1)S(1)}, bf16[12,768]{1,0:T(8,128)(2,1)S(1)}, u32[]{:S(2)}, u32[]{:S(2)}) collective-permute-start(bf16[12,768]{1,0:T(8,128)(2,1)S(1)} %collective-permute-done.5), channel_id=1, source_target_pairs={{0,4},{4,8},{8,12},{12,16},{16,20},{20,24},{24,28},{28,0},{1,5},{5... | collective-permute-start | bytes 55304 | tf_op jit(solution)/shard_map/ppermute | solution.py:52
  42.2 6.5 %collective-permute-start.7 = (bf16[12,768]{1,0:T(8,128)(2,1)S(1)}, bf16[12,768]{1,0:T(8,128)(2,1)S(1)}, u32[]{:S(2)}, u32[]{:S(2)}) collective-permute-start(bf16[12,768]{1,0:T(8,128)(2,1)S(1)} %collective-permute-done.6), channel_id=1, source_target_pairs={{0,4},{4,8},{8,12},{12,16},{16,20},{20,24},{24,28},{28,0},{1,5},{5... | collective-permute-start | bytes 55304 | tf_op jit(solution)/shard_map/ppermute | solution.py:52
  48.7 6.5 %collective-permute-start.8 = (bf16[12,768]{1,0:T(8,128)(2,1)S(1)}, bf16[12,768]{1,0:T(8,128)(2,1)S(1)}, u32[]{:S(2)}, u32[]{:S(2)}) collective-permute-start(bf16[12,768]{1,0:T(8,128)(2,1)S(1)} %collective-permute-done.7), channel_id=1, source_target_pairs={{0,4},{4,8},{8,12},{12,16},{16,20},{20,24},{24,28},{28,0},{1,5},{5... | collective-permute-start | bytes 55304 | tf_op jit(solution)/shard_map/ppermute | solution.py:52
  55.2 6.5 %collective-permute-start.9 = (bf16[12,768]{1,0:T(8,128)(2,1)S(1)}, bf16[12,768]{1,0:T(8,128)(2,1)S(1)}, u32[]{:S(2)}, u32[]{:S(2)}) collective-permute-start(bf16[12,768]{1,0:T(8,128)(2,1)S(1)} %collective-permute-done.8), channel_id=1, source_target_pairs={{0,4},{4,8},{8,12},{12,16},{16,20},{20,24},{24,28},{28,0},{1,5},{5... | collective-permute-start | bytes 55304 | tf_op jit(solution)/shard_map/ppermute | solution.py:52
  61.8 23.3 %collective-permute-start.10 = (bf16[12,768]{1,0:T(8,128)(2,1)S(1)}, bf16[12,768]{1,0:T(8,128)(2,1)S(1)}, u32[]{:S(2)}, u32[]{:S(2)}) collective-permute-start(bf16[12,768]{1,0:T(8,128)(2,1)S(1)} %collective-permute-done.9), channel_id=1, source_target_pairs={{0,4},{4,8},{8,12},{12,16},{16,20},{20,24},{24,28},{28,0},{1,5},{5... | collective-permute-start | bytes 55304 | tf_op jit(solution)/shard_map/ppermute | solution.py:52
  78.2 2.8 %slice-start = ((bf16[12,196864]{1,0:T(8,128)(2,1)}), bf16[12,196608]{1,0:T(8,128)(2,1)S(1)}, s32[]{:S(2)}) async-start(bf16[12,196864]{1,0:T(8,128)(2,1)} %tile.10), calls=%async_computation | async-start | bytes 12582912 | tf_op jit(solution)/shard_map/slice | solution.py:45
